TPU v7x, 512 devices: a whole 4x8x8 slice. The times are simulated.
512 devices in a mesh: seq: 128 (over z_hi, y, x, core), chan: 4 (over z_lo).
Axes of the slice: x: 4, y: 8, z: 8 (z_hi: 2, z_lo: 4; z = z_hi * 4 + z_lo), core: 2. Of those that a mesh axis runs over, the one named last changes fastest.
Arguments:
- residual: bfloat16 [16384, 8192], P('seq', 'chan'), may hold values from -64 to 64
- query_in: bfloat16 [16384, 8192], P('seq', 'chan'), may hold values from -6 to 6
- key_in: bfloat16 [16384, 8192], P('seq', 'chan'), may hold values from -6 to 6
- value_in: bfloat16 [16384, 8192], P('seq', 'chan'), may hold values from -6 to 6
- short_filter: float32 [3, 3, 8192], P(None, None, 'chan'), may hold values from -3.5 to 3.5
- decay_rate: float32 [16, 8192], P(None, 'chan'), may hold values from 0 to 1
- residue: float32 [16, 8192], P(None, 'chan'), may hold values from -1.5 to 1.5
- skip_gain: float32 [8192], P('chan'), may hold values from -3 to 3
- norm_gain: float32 [8192], P('chan'), may hold values from 0.1 to 1.9
Outputs:
- residual_out: bfloat16 [16384, 8192], P('seq', 'chan')
- normed: bfloat16 [16384, 8192], P('seq', 'chan')
All inputs are finite; a program needn't handle non-finite values.
Results may differ from a plain program's by a relative error of at most 0.0055.
Values may be sent and summed in bfloat16 or wider, within the bound.
No kernel may reach another device: no remote copies, remote signals or barrier semaphores. Data moves between devices by JAX's collectives and lax.ppermute only.
A program may use at most 128 MiB of HBM per device.

v0:
```python
import jax
import jax.numpy as jnp
from jax import lax
from jax.sharding import PartitionSpec as P

D = 8192
sub_block = 16
epsilon = 1e-06
highest = lax.Precision.HIGHEST


def shifted(block, axis, distance):
    devices = range(lax.axis_size(axis))
    route = [(i - distance, i) for i in devices if i - distance in devices]
    return lax.ppermute(block, axis, route)


def short_features(inputs, before, tap_weights):
    lag_rows = before.shape[0]
    token_rows = inputs.shape[0]
    extended = jnp.concatenate([before, inputs], axis=0).astype(jnp.float32)
    result = tap_weights[0][None, :] * extended[lag_rows : lag_rows + token_rows]
    for offset in range(1, lag_rows + 1):
        result = (
            result
            + tap_weights[offset][None, :]
            * extended[lag_rows - offset : lag_rows - offset + token_rows]
        )
    return result


def link_states(earlier, later):
    return (earlier[0] * later[0], later[0] * earlier[1] + later[1])


def body(
    residual, query_in, key_in, value_in, short_filter, decay_rate, residue, skip_gain, norm_gain
):
    token_rows, chan_width = residual.shape
    lag_rows = short_filter.shape[1] - 1
    tail_rows = (
        query_in[token_rows - lag_rows :],
        key_in[token_rows - lag_rows :],
        value_in[token_rows - lag_rows :],
    )
    before = shifted((tail_rows[0], tail_rows[1], tail_rows[2]), "seq", 1)
    query_side = short_features(query_in, before[0], short_filter[0])
    key_side = short_features(key_in, before[1], short_filter[1])
    value_side = short_features(value_in, before[2], short_filter[2])
    mixed = key_side * value_side
    weights = residue * jnp.sqrt(2.0 * decay_rate)
    sub_count = token_rows // sub_block
    positions = jnp.arange(sub_block, dtype=jnp.float32)
    local_taps = jnp.sum(
        weights[None] * jnp.exp(-decay_rate[None] * positions[:, None, None]), axis=1
    )
    lag_table = positions[:, None] - positions[None, :]
    one_hot = (lag_table[:, :, None] == positions[None, None, :]).astype(jnp.float32)
    toeplitz = jnp.dot(
        one_hot.reshape(sub_block * sub_block, sub_block), local_taps, precision=highest
    ).reshape(sub_block, sub_block, chan_width)
    blocks = mixed.reshape(sub_count, sub_block, chan_width)
    inside = jnp.sum(toeplitz[None, :, :, :] * blocks[:, None, :, :], axis=2)
    tail_decay = jnp.exp(-decay_rate[None] * (sub_block - 1.0 - positions)[:, None, None])
    sub_states = jnp.sum(blocks[:, :, None, :] * tail_decay[None], axis=1)
    step_decay = jnp.broadcast_to(jnp.exp(-decay_rate * sub_block)[None], sub_states.shape)
    _, running = lax.associative_scan(link_states, (step_decay, sub_states), axis=0)
    block_state = running[sub_count - 1]
    entering = jnp.concatenate([jnp.zeros_like(running[:1]), running[:-1]], axis=0)
    position = lax.axis_index("seq")
    piece = lax.all_gather(
        block_state[None].astype(jnp.bfloat16), "seq", axis=0, tiled=True
    ).astype(jnp.float32)
    members = piece.shape[0]
    sources = jnp.arange(members, dtype=jnp.int32)
    distance = position - 1 - sources
    spans = (token_rows * jnp.maximum(distance, 0)).astype(jnp.float32)
    factors = jnp.exp(-decay_rate[None] * spans[:, None, None])
    masked = jnp.where((distance >= 0)[:, None, None], factors * piece, 0.0)
    carried = jnp.zeros_like(block_state) + jnp.sum(masked, axis=0)
    sub_starts = jnp.arange(sub_count, dtype=jnp.float32) * sub_block
    entering = entering + jnp.exp(-decay_rate[None] * sub_starts[:, None, None]) * carried[None]
    readout = weights[None] * jnp.exp(-decay_rate[None] * (positions + 1.0)[:, None, None])
    across = jnp.sum(readout[None, :, :, :] * entering[:, None, :, :], axis=2)
    convolved = (inside + across).reshape(token_rows, chan_width)
    gated = query_side * (convolved + skip_gain[None, :] * mixed)
    summed = (residual.astype(jnp.float32) + gated).astype(jnp.bfloat16)
    widened = lax.optimization_barrier(summed).astype(jnp.float32)
    row_squares = lax.psum(jnp.sum(widened * widened, axis=1), "chan")
    inverse_rms = lax.rsqrt(row_squares / D + epsilon)
    normed = (widened * inverse_rms[:, None] * norm_gain[None, :]).astype(jnp.bfloat16)
    return (summed, normed)


def solution(mesh):
    in_specs = (
        P("seq", "chan"),
        P("seq", "chan"),
        P("seq", "chan"),
        P("seq", "chan"),
        P(None, None, "chan"),
        P(None, "chan"),
        P(None, "chan"),
        P("chan"),
        P("chan"),
    )
    out_specs = (P("seq", "chan"), P("seq", "chan"))
    return jax.shard_map(body, mesh=mesh, in_specs=in_specs, out_specs=out_specs, check_vma=False)
```

profile of v0, /device:TPU:2, one launch (start us, length us, event | category | flops | bytes accessed | tf_op | source)
XLA Modules:
  0.0 229.2 jit_solution(10560586186307022351)
XLA Ops:
  7.2 0.8 slice.156
  8.0 1.9 collective-permute-start.1
  9.9 0.8 slice.163
  10.7 3.5 %collective-permute-start.2 = (bf16[2,2048]{1,0:T(2,128)(2,1)S(1)}, bf16[2,2048]{1,0:T(2,128)(2,1)S(1)}, u32[]{:S(2)}, u32[]{:S(2)}) collective-permute-start(bf16[2,2048]{1,0:T(2,128)(2,1)S(1)} %slice.163), channel_id=1, source_target_pairs={{0,4},{4,8},{8,12},{12,16},{16,20},{20,24},{24,28},{28,32},{32,36}... | collective-permute-start | bytes 24584 | tf_op jit(solution)/shard_map/ppermute | solution.py:15
  14.2 1.0 fusion.24
  15.2 1.0 fusion.21
  16.3 2.4 %exponential_multiply_fusion = (f32[16,16,2048]{2,1,0:T(8,128)}, f32[16,2048]{1,0:T(8,128)S(1)}, f32[16,16,2048]{2,1,0:T(8,128)S(1)}) fusion(f32[16]{0:T(128)S(1)} %get-tuple-element.25, f32[16,2048]{1,0:T(8,128)S(1)} %get-tuple-element.13, f32[16,2048]{1,0:T(8,128)S(1)} %get-tuple-element.14, f32[16]{0:T(128)S(1)} %get-tuple-element.24), kind=kLoop, calls=%fused_computation.5 | loop fusion | flops 3112960 | bytes 4587648 | tf_op jit(solution)/shard_map/mul | solution.py:83
  18.7 1.0 fusion.17
  20.1 0.7 fusion.4
  20.7 5.8 %multiply_reduce_fusion.1 = (f32[8,16,2048]{2,1,0:T(8,128)S(1)}, f32[8,16,2048]{2,1,0:T(8,128)}) fusion(f32[16,16,2048]{2,1,0:T(8,128)S(1)} %get-tuple-element.10, f32[8,16,2048]{2,1,0:T(8,128)S(1)} %bitcast.23, f32[16,16,2048]{2,1,0:T(8,128)S(1)} %fusion.17), kind=kLoop, calls=%fused_computation.2 | loop fusion | flops 16252928 | bytes 7340032 | tf_op jit(solution)/shard_map/reduce_sum | solution.py:65
  26.6 0.8 copy-done.6
  27.6 1.5 pad.22
  29.1 1.1 add.100
  30.2 2.3 %pad.62 = f32[7,16,2048]{2,1,0:T(8,128)} pad(f32[4,16,2048]{2,1,0:T(8,128)S(1)} %add.100, f32[]{:T(128)} %constant.13.clone.1), padding=0_0_1x0_0_0x0_0_0 | pad | bytes 1441796
  32.5 1.5 add_convert_fusion
  34.1 0.8 slice.149
  34.9 2.1 collective-permute-start
  37.1 1.1 fusion.13
  38.2 2.4 %pad.25 = f32[8,16,2048]{2,1,0:T(8,128)} pad(f32[4,16,2048]{2,1,0:T(8,128)S(1)} %add.100, f32[]{:T(128)} %constant.13.clone.1), padding=1_0_1x0_0_0x0_0_0 | pad | bytes 1572868 | tf_op jit(solution)/shard_map/pad | solution.py:67
  40.5 2.4 %pad.24 = f32[8,16,2048]{2,1,0:T(8,128)} pad(f32[4,16,2048]{2,1,0:T(8,128)S(1)} %pad_maximum_fusion, f32[]{:T(128)} %constant.13.clone.1), padding=0_1_1x0_0_0x0_0_0 | pad | bytes 1572868 | tf_op jit(solution)/shard_map/pad | solution.py:67
  43.0 1.3 maximum_convert_fusion
  44.3 1.0 slice_add_fusion
  45.4 151.6 %all-gather.2.cloned.1.call-done = bf16[128,16,2048]{2,1,0:T(8,128)(2,1)} async-done(((bf16[1,16,2048]{2,1,0:T(8,128)(2,1)}), bf16[128,16,2048]{2,1,0:T(8,128)(2,1)}) %all-gather.2.cloned.1.call-update) | async-done | bytes 8388624 | tf_op jit(solution)/shard_map/all_gather | solution.py:71
  197.0 7.1 %select_reduce_fusion = f32[16,2048]{1,0:T(8,128)S(1)} fusion(bf16[128,16,2048]{2,1,0:T(8,128)(2,1)} %all-gather.2.cloned.1.call-done, f32[128]{0:T(128)S(1)} %multiply_convert_fusion, f32[16,2048]{1,0:T(8,128)S(1)} %get-tuple-element.13, pred[128]{0:T(512)(128)(4,1)S(1)} %fusion.20), kind=kLoop, calls=%fused_computation.1 | loop fusion | flops 20938752 | bytes 8651392 | tf_op jit(solution)/shard_map/reduce_sum | solution.py:80
  204.1 0.2 multiply_add_fusion
  204.3 1.3 copy-done
  205.6 4.2 %multiply_reduce_fusion = f32[8,16,2048]{2,1,0:T(8,128)S(1)} fusion(f32[8,16,2048]{2,1,0:T(8,128)S(1)} %multiply_add_fusion, f32[16,16,2048]{2,1,0:T(8,128)S(1)} %copy-done), kind=kLoop, calls=%fused_computation | loop fusion | flops 8126464 | bytes 4194304 | tf_op jit(solution)/shard_map/reduce_sum | solution.py:84
  210.0 0.9 copy-done.9
  210.9 0.5 fusion.11
  211.4 0.2 fusion
  211.6 9.7 %psum.7 = f32[128]{0:T(128)S(1)} all-reduce(f32[128]{0:T(128)S(1)} %fusion), channel_id=1, replica_groups=mesh['seq'=128,'chan'=4] {'chan'}, use_global_device_ids=true, to_apply=%region_6.7 | all-reduce | flops 128 | bytes 1024 | tf_op jit(solution)/shard_map/psum | solution.py:89
  221.3 1.0 fusion.2
  (44 shorter events, 1.0 us)
Async XLA Ops:
  7.2 189.8 %all-gather.2.cloned.1.call-start = ((), (), s32[]{:S(2)}) async-start(), calls=%async_computation | async-start | bytes 8454144 | tf_op jit(solution)/shard_map/all_gather | solution.py:71
  8.0 11.7 %collective-permute-start.1 = (bf16[2,2048]{1,0:T(2,128)(2,1)S(1)}, bf16[2,2048]{1,0:T(2,128)(2,1)S(1)}, u32[]{:S(2)}, u32[]{:S(2)}) collective-permute-start(bf16[2,2048]{1,0:T(2,128)(2,1)S(1)} %slice.156), channel_id=1, source_target_pairs={{0,4},{4,8},{8,12},{12,16},{16,20},{20,24},{24,28},{28,32},{32,36}... | collective-permute-start | bytes 24584 | tf_op jit(solution)/shard_map/ppermute | solution.py:15
  10.7 9.2 %collective-permute-start.2 = (bf16[2,2048]{1,0:T(2,128)(2,1)S(1)}, bf16[2,2048]{1,0:T(2,128)(2,1)S(1)}, u32[]{:S(2)}, u32[]{:S(2)}) collective-permute-start(bf16[2,2048]{1,0:T(2,128)(2,1)S(1)} %slice.163), channel_id=1, source_target_pairs={{0,4},{4,8},{8,12},{12,16},{16,20},{20,24},{24,28},{28,32},{32,36}... | collective-permute-start | bytes 24584 | tf_op jit(solution)/shard_map/ppermute | solution.py:15
  18.7 1.0 copy-start.7
  18.7 1.2 copy-start.8
  26.5 0.9 copy-start.6
  34.9 8.1 %collective-permute-start = (bf16[2,2048]{1,0:T(2,128)(2,1)S(1)}, bf16[2,2048]{1,0:T(2,128)(2,1)S(1)}, u32[]{:S(2)}, u32[]{:S(2)}) collective-permute-start(bf16[2,2048]{1,0:T(2,128)(2,1)S(1)} %slice.149), channel_id=1, source_target_pairs={{0,4},{4,8},{8,12},{12,16},{16,20},{20,24},{24,28},{28,32},{32,36}... | collective-permute-start | bytes 24584 | tf_op jit(solution)/shard_map/ppermute | solution.py:15
  40.5 3.7 %copy-start.3 = (f32[8,16,2048]{2,1,0:T(8,128)S(1)}, f32[8,16,2048]{2,1,0:T(8,128)}, u32[]{:S(2)}) copy-start(f32[8,16,2048]{2,1,0:T(8,128)} %pad.25) | copy-start | bytes 3145732
  43.0 1.4 copy-start.4
  45.4 158.7 %copy-start.5 = (f32[7,16,2048]{2,1,0:T(8,128)S(1)}, f32[7,16,2048]{2,1,0:T(8,128)}, u32[]{:S(2)}) copy-start(f32[7,16,2048]{2,1,0:T(8,128)} %slice_add_fusion) | copy-start | bytes 2752516
  204.0 1.6 copy-start
  205.6 4.2 %copy-start.2 = (f32[8,16,2048]{2,1,0:T(8,128)S(1)}, f32[8,16,2048]{2,1,0:T(8,128)}, u32[]{:S(2)}) copy-start(f32[8,16,2048]{2,1,0:T(8,128)} %get-tuple-element.3) | copy-start | bytes 3145732
  209.8 1.0 copy-start.9
  209.9 1.0 copy-start.10
  210.9 10.4 %copy-start.11 = (f32[2048]{0:T(1024)S(1)}, f32[2048]{0:T(1024)}, u32[]{:S(2)}) copy-start(f32[2048]{0:T(1024)} %param.17) | copy-start | bytes 24580
  211.4 10.9 %copy-start.1 = (bf16[128,2048]{1,0:T(8,128)(2,1)}, bf16[128,2048]{1,0:T(8,128)(2,1)S(1)}, u32[]{:S(2)}) copy-start(bf16[128,2048]{1,0:T(8,128)(2,1)S(1)} %fusion.11) | copy-start | bytes 1572868
Sparse Core Ops, SparseCore 0:
  34.2 162.6 all-gather.1
where the time goes:
time: 230 us; the launch traced here: 229 us
  waiting for transfers between devices  152 us (66%)
  other arithmetic  29.9 us (13%)
  local copies, waits for them, and re-layouts  15.1 us (7%)
  between operations  14.3 us (6%)
  blocking collectives  9.68 us (4%)
  starting transfers between devices  7.56 us (3%)
    all_gather x1, waiting for transfers between devices, body(): lax.all_gather(block_state[None].astype(jnp.bfloat16), 'seq', axis=0, til...  152 us
    psum x1, blocking collectives, body(): row_squares = lax.psum(jnp.sum(widened * widened, axis=1), 'chan')  9.68 us
    ppermute x3, starting transfers between devices, shifted(): return lax.ppermute(block, axis, route)  7.52 us
    reduce_sum x1, other arithmetic, body(): carried = jnp.zeros_like(block_state) + jnp.sum(masked, axis=0)  7.07 us
    pad x4, local copies, waits for them, and re-layouts, body(): lax.associative_scan(link_states, (step_decay, sub_states), axis=0)  6.35 us
    reduce_sum x1, other arithmetic, body(): sub_states = jnp.sum(blocks[:, :, None, :] * tail_decay[None], axis=1)  5.81 us
    unnamed x25, local copies, waits for them, and re-layouts  5.43 us
  transfers between devices with their start and end apart: 4, of which 1 were waited for; matrix products, arithmetic and copies ran while one was open for 7% of the time, Pallas kernels for 0%

commit v1 on v0

--- a/solution.py
+++ b/solution.py
@@ -68,9 +68,14 @@
     block_state = running[sub_count - 1]
     entering = jnp.concatenate([jnp.zeros_like(running[:1]), running[:-1]], axis=0)
     position = lax.axis_index("seq")
-    piece = lax.all_gather(
-        block_state[None].astype(jnp.bfloat16), "seq", axis=0, tiled=True
-    ).astype(jnp.float32)
+
+    def derive_tasks(sheet):
+        z1 = jax.lax.all_to_all(
+            jnp.stack([sheet for _ in range(jax.lax.axis_size("seq"))], axis=0), "seq", 0, 0
+        )
+        return jnp.concatenate(z1, 0)
+
+    piece = derive_tasks(block_state[None].astype(jnp.bfloat16)).astype(jnp.float32)
     members = piece.shape[0]
     sources = jnp.arange(members, dtype=jnp.int32)
     distance = position - 1 - sources

time: 230 us -> 285 us (1.24)
  the two profiles are of different devices: /device:TPU:2 before, /device:TPU:8 now
where the time goes in v1:
time: 285 us; the launch traced here: 284 us
  waiting for transfers between devices  198 us (69%)
  other arithmetic  29.2 us (10%)
  starting transfers between devices  27.6 us (10%)
  local copies, waits for them, and re-layouts  19.3 us (7%)
  blocking collectives  8.37 us (3%)
    ppermute x3, waiting for transfers between devices, shifted(): return lax.ppermute(block, axis, route)  175 us
    all_to_all x1, waiting for transfers between devices, derive_tasks(): jax.lax.all_to_all(jnp.stack([sheet for _ in range(jax.lax.axis_size('seq...  23.2 us
    all_to_all x1, starting transfers between devices, derive_tasks(): jax.lax.all_to_all(jnp.stack([sheet for _ in range(jax.lax.axis_size('seq...  20 us
    psum x1, blocking collectives, body(): row_squares = lax.psum(jnp.sum(widened * widened, axis=1), 'chan')  8.37 us
    ppermute x3, starting transfers between devices, shifted(): return lax.ppermute(block, axis, route)  7.63 us
    reduce_sum x1, other arithmetic, body(): carried = jnp.zeros_like(block_state) + jnp.sum(masked, axis=0)  7.08 us
    pad x4, local copies, waits for them, and re-layouts, body(): lax.associative_scan(link_states, (step_decay, sub_states), axis=0)  6.26 us
    reduce_sum x1, other arithmetic, body(): sub_states = jnp.sum(blocks[:, :, None, :] * tail_decay[None], axis=1)  5.83 us
  transfers between devices with their start and end apart: 4, of which 2 were waited for; matrix products, arithmetic and copies ran while one was open for 5% of the time, Pallas kernels for 0%

profile of v1, /device:TPU:8, one launch (start us, length us, event | category | flops | bytes accessed | tf_op | source)
XLA Modules:
  0.0 284.4 jit_solution(1011600190533010923)
XLA Ops:
  0.6 0.8 slice.163
  1.4 1.9 collective-permute-start.2
  3.3 0.8 slice.156
  4.1 3.5 %collective-permute-start.1 = (bf16[2,2048]{1,0:T(2,128)(2,1)S(1)}, bf16[2,2048]{1,0:T(2,128)(2,1)S(1)}, u32[]{:S(2)}, u32[]{:S(2)}) collective-permute-start(bf16[2,2048]{1,0:T(2,128)(2,1)S(1)} %slice.156), channel_id=1, source_target_pairs={{0,4},{4,8},{8,12},{12,16},{16,20},{20,24},{24,28},{28,32},{32,36}... | collective-permute-start | bytes 24584 | tf_op jit(solution)/shard_map/ppermute | solution.py:15
  7.6 1.1 fusion.27
  8.7 1.0 fusion.24
  9.7 2.4 exponential_multiply_fusion
  12.1 1.0 fusion.19
  13.5 0.7 fusion.6
  14.2 5.8 %multiply_reduce_fusion.1 = (f32[8,16,2048]{2,1,0:T(8,128)S(1)}, f32[8,16,2048]{2,1,0:T(8,128)}) fusion(f32[16,16,2048]{2,1,0:T(8,128)S(1)} %get-tuple-element.10, f32[8,16,2048]{2,1,0:T(8,128)S(1)} %bitcast.28, f32[16,16,2048]{2,1,0:T(8,128)S(1)} %fusion.19), kind=kLoop, calls=%fused_computation.4 | loop fusion | flops 16252928 | bytes 7340032 | tf_op jit(solution)/shard_map/reduce_sum | solution.py:65
  20.1 0.8 copy-done.6
  21.1 1.5 pad.23
  22.6 1.1 add.100
  23.7 2.3 pad.62
  26.0 0.9 fusion.21
  26.9 4.3 %stack.2 = bf16[128,1,16,2048]{3,2,1,0:T(8,128)(2,1)} broadcast(bf16[16,2048]{1,0:T(8,128)(2,1)S(1)} %fusion.21), dimensions={2,3} | broadcast | bytes 8454144 | tf_op jit(solution)/shard_map/stack | solution.py:74
  31.2 20.0 %all-to-all-start = ((bf16[128,1,16,2048]{3,2,1,0:T(8,128)(2,1)}), bf16[128,1,16,2048]{3,2,1,0:T(8,128)(2,1)}, u32[]{:S(2)}, u32[]{:S(2)}) async-start(bf16[128,1,16,2048]{3,2,1,0:T(8,128)(2,1)} %stack.2), calls=%async_computation | async-start | bytes 16777216 | tf_op jit(solution)/shard_map/all_to_all | solution.py:73
  51.2 0.8 slice.149
  52.0 2.2 collective-permute-start
  54.2 1.1 fusion.15
  55.4 2.4 pad.25
  57.7 2.3 pad.24
  60.1 174.8 %collective-permute-done = bf16[2,2048]{1,0:T(2,128)(2,1)S(1)} collective-permute-done((bf16[2,2048]{1,0:T(2,128)(2,1)S(1)}, bf16[2,2048]{1,0:T(2,128)(2,1)S(1)}, u32[]{:S(2)}, u32[]{:S(2)}) %collective-permute-start) | collective-permute-done | bytes 8224 | tf_op jit(solution)/shard_map/ppermute | solution.py:15
  234.9 1.2 maximum_convert_fusion
  236.1 1.0 slice_add_fusion
  237.1 23.2 %all-to-all-done = bf16[128,1,16,2048]{3,2,1,0:T(8,128)(2,1)} async-done(((bf16[128,1,16,2048]{3,2,1,0:T(8,128)(2,1)}), bf16[128,1,16,2048]{3,2,1,0:T(8,128)(2,1)}, u32[]{:S(2)}, u32[]{:S(2)}) %all-to-all-start) | async-done | bytes 8388640 | tf_op jit(solution)/shard_map/all_to_all | solution.py:73
  260.3 7.1 %fusion.1 = f32[16,2048]{1,0:T(8,128)S(1)} fusion(bf16[128,1,16,2048]{3,2,1,0:T(8,128)(2,1)} %all-to-all-done, f32[128]{0:T(128)S(1)} %multiply_convert_fusion, f32[16,2048]{1,0:T(8,128)S(1)} %get-tuple-element.13, pred[128]{0:T(512)(128)(4,1)S(1)} %fusion.23), kind=kLoop, calls=%fused_computation.2 | loop fusion | flops 20938752 | bytes 8651392 | tf_op jit(solution)/shard_map/reduce_sum | solution.py:85
  267.7 1.3 copy-done
  269.0 4.2 %multiply_reduce_fusion = f32[8,16,2048]{2,1,0:T(8,128)S(1)} fusion(f32[8,16,2048]{2,1,0:T(8,128)S(1)} %multiply_add_fusion, f32[16,16,2048]{2,1,0:T(8,128)S(1)} %copy-done), kind=kLoop, calls=%fused_computation.3 | loop fusion | flops 8126464 | bytes 4194304 | tf_op jit(solution)/shard_map/reduce_sum | solution.py:89
  273.4 0.9 copy-done.9
  275.0 8.4 %psum.7 = f32[128]{0:T(128)S(1)} all-reduce(f32[128]{0:T(128)S(1)} %fusion.2), channel_id=1, replica_groups=mesh['seq'=128,'chan'=4] {'chan'}, use_global_device_ids=true, to_apply=%region_6.7 | all-reduce | flops 128 | bytes 1024 | tf_op jit(solution)/shard_map/psum | solution.py:94
  283.4 1.0 fusion.4
  (44 shorter events, 1.8 us)
Async XLA Ops:
  1.4 11.8 %collective-permute-start.2 = (bf16[2,2048]{1,0:T(2,128)(2,1)S(1)}, bf16[2,2048]{1,0:T(2,128)(2,1)S(1)}, u32[]{:S(2)}, u32[]{:S(2)}) collective-permute-start(bf16[2,2048]{1,0:T(2,128)(2,1)S(1)} %slice.163), channel_id=1, source_target_pairs={{0,4},{4,8},{8,12},{12,16},{16,20},{20,24},{24,28},{28,32},{32,36}... | collective-permute-start | bytes 24584 | tf_op jit(solution)/shard_map/ppermute | solution.py:15
  4.1 9.2 %collective-permute-start.1 = (bf16[2,2048]{1,0:T(2,128)(2,1)S(1)}, bf16[2,2048]{1,0:T(2,128)(2,1)S(1)}, u32[]{:S(2)}, u32[]{:S(2)}) collective-permute-start(bf16[2,2048]{1,0:T(2,128)(2,1)S(1)} %slice.156), channel_id=1, source_target_pairs={{0,4},{4,8},{8,12},{12,16},{16,20},{20,24},{24,28},{28,32},{32,36}... | collective-permute-start | bytes 24584 | tf_op jit(solution)/shard_map/ppermute | solution.py:15
  12.1 1.0 copy-start.7
  12.1 1.2 copy-start.8
  20.0 0.9 copy-start.6
  31.2 229.1 %all-to-all-start = ((bf16[128,1,16,2048]{3,2,1,0:T(8,128)(2,1)}), bf16[128,1,16,2048]{3,2,1,0:T(8,128)(2,1)}, u32[]{:S(2)}, u32[]{:S(2)}) async-start(bf16[128,1,16,2048]{3,2,1,0:T(8,128)(2,1)} %stack.2), calls=%async_computation | async-start | bytes 16777216 | tf_op jit(solution)/shard_map/all_to_all | solution.py:73
  52.0 182.9 %collective-permute-start = (bf16[2,2048]{1,0:T(2,128)(2,1)S(1)}, bf16[2,2048]{1,0:T(2,128)(2,1)S(1)}, u32[]{:S(2)}, u32[]{:S(2)}) collective-permute-start(bf16[2,2048]{1,0:T(2,128)(2,1)S(1)} %slice.149), channel_id=1, source_target_pairs={{0,4},{4,8},{8,12},{12,16},{16,20},{20,24},{24,28},{28,32},{32,36}... | collective-permute-start | bytes 24584 | tf_op jit(solution)/shard_map/ppermute | solution.py:15
  57.7 178.3 %copy-start.3 = (f32[8,16,2048]{2,1,0:T(8,128)S(1)}, f32[8,16,2048]{2,1,0:T(8,128)}, u32[]{:S(2)}) copy-start(f32[8,16,2048]{2,1,0:T(8,128)} %pad.25) | copy-start | bytes 3145732
  60.1 176.0 %copy-start.4 = (f32[8,16,2048]{2,1,0:T(8,128)S(1)}, f32[8,16,2048]{2,1,0:T(8,128)}, u32[]{:S(2)}) copy-start(f32[8,16,2048]{2,1,0:T(8,128)} %pad.24) | copy-start | bytes 3145732
  237.1 30.3 %copy-start.5 = (f32[7,16,2048]{2,1,0:T(8,128)S(1)}, f32[7,16,2048]{2,1,0:T(8,128)}, u32[]{:S(2)}) copy-start(f32[7,16,2048]{2,1,0:T(8,128)} %slice_add_fusion) | copy-start | bytes 2752516
  267.4 1.6 copy-start
  269.0 4.2 %copy-start.2 = (f32[8,16,2048]{2,1,0:T(8,128)S(1)}, f32[8,16,2048]{2,1,0:T(8,128)}, u32[]{:S(2)}) copy-start(f32[8,16,2048]{2,1,0:T(8,128)} %get-tuple-element.3) | copy-start | bytes 3145732
  273.2 1.0 copy-start.9
  273.2 1.0 copy-start.10
  274.3 9.1 %copy-start.11 = (f32[2048]{0:T(1024)S(1)}, f32[2048]{0:T(1024)}, u32[]{:S(2)}) copy-start(f32[2048]{0:T(1024)} %param.17) | copy-start | bytes 24580
  274.8 9.6 %copy-start.1 = (bf16[128,2048]{1,0:T(8,128)(2,1)}, bf16[128,2048]{1,0:T(8,128)(2,1)S(1)}, u32[]{:S(2)}) copy-start(bf16[128,2048]{1,0:T(8,128)(2,1)S(1)} %fusion.13) | copy-start | bytes 1572868
